TPU v7x, 32 devices: a whole 2x2x4 slice. The times are simulated.
32 devices in a mesh: row: 4 (over y, x), col: 8 (over z, core).
Axes of the slice: x: 2, y: 2, z: 4, core: 2. Of those that a mesh axis runs over, the one named last changes fastest.
Arguments:
- noise: float32 [2048, 3072], P('row', 'col'), may hold values from -30 to 30
- images: float32 [6144, 3072], P('col', 'row'), may hold values from -6 to 6
- time_index: int32 [2048], P('row'), may hold values from 0 to 999
- w_in: float32 [3072, 3072], P(None, 'col'), may hold values from -0.109375 to 0.109375
- time_gain: float32 [3072], P('col'), may hold values from -5 to 5
- w_out: float32 [3072, 3072], P('col'), may hold values from -0.109375 to 0.109375
Outputs:
- targets: float32 [2048, 3072], P('row', 'col')
- row_pot: float32 [2048], P('row')
- col_pot: float32 [6144], P('col')
- grad_in: float32 [3072, 3072], P('row', 'col')
- grad_time: float32 [3072], P('col')
- grad_out: float32 [3072, 3072], P('col', 'row')
- mse: float32 [], replicated
All inputs are finite; a program needn't handle non-finite values.
Results may differ from a plain program's by a relative error of at most 0.0003.
Values sent between devices are 32-bit elements; how exact they have to be, the bound alone decides.
A program may use at most 128 MiB of HBM per device.

v0:
```python
import jax
import jax.numpy as jnp
from jax import lax
from jax.sharding import PartitionSpec as P

ITERS = 2
TIMES = 1000
EPSILON = 0.01


def merged(array, axis, combine):
    everything = jax.tree.map(lambda part: lax.all_gather(part, axis), array)
    first = jax.tree.map(lambda part: part[0], everything)

    def hop(k, so_far):
        return combine(so_far, jax.tree.map(lambda part: part[k], everything))

    return lax.fori_loop(1, lax.axis_size(axis), hop, first)


def joined(left_pair, right_pair):
    peak = jnp.maximum(left_pair[0], right_pair[0])
    total = left_pair[1] * jnp.exp(left_pair[0] - peak) + right_pair[1] * jnp.exp(
        right_pair[0] - peak
    )
    return (peak, total)


def over_images(logits):
    local_peak = jnp.max(logits, axis=1)
    local_total = jnp.sum(jnp.exp(logits - local_peak[:, None]), axis=1)
    peak, total = merged((local_peak, local_total), "col", joined)
    return (peak, total)


def over_noise(logits):
    local_peak = jnp.max(logits, axis=0)
    local_total = jnp.sum(jnp.exp(logits - local_peak[None, :]), axis=0)
    peak, total = merged((local_peak, local_total), "row", joined)
    return (peak, total)


def body(noise, images, time_index, w_in, time_gain, w_out):
    highest = lax.Precision.HIGHEST
    full_noise = lax.all_gather(noise, "col", axis=1, tiled=True)
    full_images = lax.all_gather(images, "row", axis=1, tiled=True)
    width = full_noise.shape[1]
    noise_count = full_noise.shape[0] * lax.axis_size("row")
    image_count = full_images.shape[0] * lax.axis_size("col")
    noise_norms = jnp.sum(full_noise * full_noise, axis=1)
    image_norms = jnp.sum(full_images * full_images, axis=1)
    cross = lax.dot_general(
        full_noise,
        full_images,
        (((1,), (1,)), ((), ())),
        precision=highest,
        preferred_element_type=jnp.float32,
    )
    scaled = (noise_norms[:, None] + image_norms[None, :] - 2.0 * cross) / (width * EPSILON)
    col_pot = jnp.zeros((full_images.shape[0],), jnp.float32)
    row_pot = jnp.zeros((full_noise.shape[0],), jnp.float32)
    for iteration in range(ITERS):
        peak, total = over_images(col_pot[None, :] - scaled)
        row_pot = jnp.log(jnp.float32(image_count)) - (jnp.log(total) + peak)
        peak, total = over_noise(row_pot[:, None] - scaled)
        col_pot = jnp.log(jnp.float32(noise_count)) - (jnp.log(total) + peak)
    logits = col_pot[None, :] - scaled
    peak, total = over_images(logits)
    weights = jnp.exp(logits - (jnp.log(total) + peak)[:, None])
    partial_value = jnp.dot(
        weights, full_images, precision=highest, preferred_element_type=jnp.float32
    )
    slice_width = noise.shape[1]
    slice_start = lax.axis_index("col") * slice_width
    whole_targets = lax.psum(partial_value, "col")
    targets = lax.dynamic_slice_in_dim(whole_targets, slice_start, slice_width, 1)
    fraction = (time_index.astype(jnp.float32) + 0.5) / TIMES
    mixed = (1.0 - fraction)[:, None] * full_noise + fraction[:, None] * whole_targets
    velocity = whole_targets - full_noise
    pre = (
        jnp.dot(mixed, w_in, precision=highest, preferred_element_type=jnp.float32)
        + fraction[:, None] * time_gain[None, :]
    )
    sigma = jax.nn.sigmoid(pre)
    hidden = pre * sigma
    part_out = jnp.dot(hidden, w_out, precision=highest, preferred_element_type=jnp.float32)
    out = lax.psum(part_out, "col")
    diff = out - velocity
    squared = jnp.sum(diff * diff)
    slope = diff / jnp.sqrt(jnp.float32(noise_count))
    local_out = lax.dot_general(
        hidden,
        slope,
        (((0,), (0,)), ((), ())),
        precision=highest,
        preferred_element_type=jnp.float32,
    )
    back = lax.dot_general(
        slope,
        w_out,
        (((1,), (1,)), ((), ())),
        precision=highest,
        preferred_element_type=jnp.float32,
    )
    dpre = back * sigma * (1.0 + pre * (1.0 - sigma))
    local_in = lax.dot_general(
        mixed, dpre, (((0,), (0,)), ((), ())), precision=highest, preferred_element_type=jnp.float32
    )
    local_time = jnp.sum(fraction[:, None] * dpre, axis=0)
    grad_in, grad_out = (
        lax.psum_scatter(local_in, "row", scatter_dimension=0, tiled=True),
        lax.psum_scatter(local_out, "row", scatter_dimension=1, tiled=True),
    )
    grad_time, squared_all = lax.psum((local_time, squared), "row")
    mse = squared_all / (noise_count * width)
    return (targets, row_pot, col_pot, grad_in, grad_time, grad_out, mse)


def solution(mesh):
    placed = (P("row", "col"), P("col", "row"), P("row"), P(None, "col"), P("col"), P("col", None))
    return jax.shard_map(
        body,
        mesh=mesh,
        in_specs=placed,
        out_specs=(
            P("row", "col"),
            P("row"),
            P("col"),
            P("row", "col"),
            P("col"),
            P("col", "row"),
            P(),
        ),
        check_vma=False,
    )
```

profile of v0, /device:TPU:0, one launch (start us, length us, event | category | flops | bytes accessed | tf_op | source)
XLA Modules:
  0.0 786.1 jit_solution(18099109052659360453)
XLA Ops:
  8.7 68.3 %all-gather.23.cloned.1.call-done = f32[512,3072]{1,0:T(8,128)} async-done(((f32[512,384]{1,0:T(8,128)}), f32[512,3072]{1,0:T(8,128)}) %all-gather.23.cloned.1.call-update) | async-done | bytes 6291472 | tf_op jit(solution)/shard_map/all_gather | solution.py:45
  77.0 3.3 multiply_reduce_fusion.2
  80.3 93.5 %all-gather.25.cloned.1.call-done = f32[768,3072]{1,0:T(8,128)} async-done(((f32[768,768]{1,0:T(8,128)}), f32[768,3072]{1,0:T(8,128)}) %all-gather.25.cloned.1.call-update) | async-done | bytes 9437200 | tf_op jit(solution)/shard_map/all_gather | solution.py:46
  173.8 4.5 multiply_reduce_fusion
  178.3 1.0 copy-done
  179.2 18.3 %subtract_reduce_fusion.3 = (f32[512]{0:T(512)S(1)}, f32[512,768]{1,0:T(8,128)S(1)}) fusion(f32[512,3072]{1,0:T(8,128)S(1)} %copy-done, f32[768,3072]{1,0:T(8,128)} %all-gather.25.cloned.1.call-done, f32[768]{0:T(1024)S(1)} %multiply_reduce_fusion, f32[512]{0:T(512)S(1)} %multiply_reduce_fusion.2), kind=kOutput, calls=%fused_computation.38 | convolution fusion | flops 14497873920 | bytes 17308672 | tf_op jit(solution)/shard_map/dot_general | solution.py:52
  197.9 12.8 %all-gather.11 = f32[8,1,512]{2,1,0:T(1,128)S(1)} all-gather(f32[1,1,512]{2,1,0:T(1,128)S(1)} %bitcast.95), channel_id=3, replica_groups=mesh['row'=4,'col'=8] {'col'}, dimensions={0}, use_global_device_ids=true | all-gather | bytes 18432 | tf_op jit(solution)/shard_map/all_gather | solution.py:12
  210.8 12.8 %all-gather.10 = f32[8,1,512]{2,1,0:T(1,128)S(1)} all-gather(f32[1,1,512]{2,1,0:T(1,128)S(1)} %bitcast.93), channel_id=2, replica_groups=mesh['row'=4,'col'=8] {'col'}, dimensions={0}, use_global_device_ids=true | all-gather | bytes 18432 | tf_op jit(solution)/shard_map/all_gather | solution.py:12
  224.5 8.1 %all-gather.13 = f32[4,1,768]{2,1,0:T(1,128)S(1)} all-gather(f32[1,1,768]{2,1,0:T(1,128)S(1)} %reshape.65), channel_id=5, replica_groups=mesh['row'=4,'col'=8] {'row'}, dimensions={0}, use_global_device_ids=true | all-gather | bytes 15360 | tf_op jit(solution)/shard_map/all_gather | solution.py:12
  232.6 7.2 all-gather.12
  240.7 12.8 %all-gather.15 = f32[8,1,512]{2,1,0:T(1,128)S(1)} all-gather(f32[1,1,512]{2,1,0:T(1,128)S(1)} %bitcast.94), channel_id=7, replica_groups=mesh['row'=4,'col'=8] {'col'}, dimensions={0}, use_global_device_ids=true | all-gather | bytes 18432 | tf_op jit(solution)/shard_map/all_gather | solution.py:12
  253.5 12.8 %all-gather.14 = f32[8,1,512]{2,1,0:T(1,128)S(1)} all-gather(f32[1,1,512]{2,1,0:T(1,128)S(1)} %bitcast.91), channel_id=6, replica_groups=mesh['row'=4,'col'=8] {'col'}, dimensions={0}, use_global_device_ids=true | all-gather | bytes 18432 | tf_op jit(solution)/shard_map/all_gather | solution.py:12
  267.2 8.1 %all-gather.17 = f32[4,1,768]{2,1,0:T(1,128)S(1)} all-gather(f32[1,1,768]{2,1,0:T(1,128)S(1)} %reshape.73), channel_id=9, replica_groups=mesh['row'=4,'col'=8] {'row'}, dimensions={0}, use_global_device_ids=true | all-gather | bytes 15360 | tf_op jit(solution)/shard_map/all_gather | solution.py:12
  275.4 18.3 %all-gather.16 = f32[4,1,768]{2,1,0:T(1,128)S(1)} all-gather(f32[1,1,768]{2,1,0:T(1,128)S(1)} %reshape.71), channel_id=8, replica_groups=mesh['row'=4,'col'=8] {'row'}, dimensions={0}, use_global_device_ids=true | all-gather | bytes 15360 | tf_op jit(solution)/shard_map/all_gather | solution.py:12
  294.6 12.8 %all-gather.19 = f32[8,1,512]{2,1,0:T(1,128)S(1)} all-gather(f32[1,1,512]{2,1,0:T(1,128)S(1)} %bitcast.96), channel_id=11, replica_groups=mesh['row'=4,'col'=8] {'col'}, dimensions={0}, use_global_device_ids=true | all-gather | bytes 18432 | tf_op jit(solution)/shard_map/all_gather | solution.py:12
  307.3 12.8 %all-gather.18 = f32[8,1,512]{2,1,0:T(1,128)S(1)} all-gather(f32[1,1,512]{2,1,0:T(1,128)S(1)} %bitcast.92), channel_id=10, replica_groups=mesh['row'=4,'col'=8] {'col'}, dimensions={0}, use_global_device_ids=true | all-gather | bytes 18432 | tf_op jit(solution)/shard_map/all_gather | solution.py:12
  320.5 19.3 %fusion.6 = f32[512,3072]{1,0:T(8,128)} fusion(f32[768,3072]{1,0:T(8,128)} %all-gather.25.cloned.1.call-done, f32[512,768]{1,0:T(8,128)S(1)} %get-tuple-element.759, f32[512]{0:T(512)S(1)} %log_add_fusion, f32[768]{0:T(1024)S(1)} %add_subtract_fusion), kind=kOutput, calls=%fused_computation.26 | convolution fusion | flops 14496301056 | bytes 17306624 | tf_op jit(solution)/shard_map/dot_general | solution.py:70
  340.4 133.1 %all-reduce.4.cloned.1.call-done = f32[512,3072]{1,0:T(8,128)} async-done(((f32[512,3072]{1,0:T(8,128)}), f32[512,3072]{1,0:T(8,128)}) %all-reduce.4.cloned.1.call-update) | async-done | bytes 6291472 | tf_op jit(solution)/shard_map/psum | solution.py:75
  473.6 14.6 %convolution_add_fusion = f32[512,384]{1,0:T(8,128)S(1)} fusion(f32[3072,384]{1,0:T(8,128)} %param.19, f32[384]{0:T(512)S(1)} %copy-done.7, f32[512]{0:T(512)S(1)} %get-tuple-element.757, f32[512,3072]{1,0:T(8,128)} %all-reduce.4.cloned.1.call-done, f32[512,3072]{1,0:T(8,128)} %all-gather.23.cloned.1.call-done, f32[512]{0:T(512)S(1)} %get-tuple-element.756), kind=kOutput, calls=%fused_computation.43 | convolution fusion | flops 7252869120 | bytes 18093568 | tf_op jit(solution)/shard_map/dot_general | solution.py:81
  488.2 0.9 copy-done.2
  489.1 12.0 %fusion.20 = f32[512,3072]{1,0:T(8,128)} fusion(f32[384,3072]{1,0:T(8,128)S(1)} %bitcast.68, f32[512,384]{1,0:T(8,128)S(1)} %convolution_add_fusion), kind=kOutput, calls=%fused_computation.49 | convolution fusion | flops 7248543744 | bytes 11796480 | tf_op jit(solution)/shard_map/dot_general | solution.py:86
  501.4 136.0 %all-reduce.6.cloned.1.call-done = f32[512,3072]{1,0:T(8,128)} async-done(((f32[512,3072]{1,0:T(8,128)}), f32[512,3072]{1,0:T(8,128)}) %all-reduce.6.cloned.1.call-update) | async-done | bytes 6291472 | tf_op jit(solution)/shard_map/psum | solution.py:87
  637.3 9.5 %multiply_reduce_fusion.1 = (f32[]{:T(128)}, f32[512,3072]{1,0:T(8,128)S(1)}) fusion(f32[512,3072]{1,0:T(8,128)} %all-reduce.6.cloned.1.call-done, f32[512,3072]{1,0:T(8,128)} %all-reduce.4.cloned.1.call-done, f32[512,3072]{1,0:T(8,128)} %all-gather.23.cloned.1.call-done), kind=kLoop, calls=%fused_computation.16 | loop fusion | flops 6291455 | bytes 25165828 | tf_op jit(solution)/shard_map/reduce_sum | solution.py:89
  646.8 2.6 copy-done.1
  649.4 10.6 %fusion = f32[384,3072]{1,0:T(8,128)} fusion(f32[512,3072]{1,0:T(8,128)S(1)} %get-tuple-element.745, f32[512,384]{1,0:T(8,128)} %copy-done.2), kind=kOutput, calls=%fused_computation.20 | convolution fusion | flops 7250116608 | bytes 11796480 | tf_op jit(solution)/shard_map/dot_general | solution.py:91
  660.4 0.8 copy-done.3
  661.2 14.1 %multiply_reduce_fusion.3 = (f32[384]{0:T(512)S(1)}, f32[512,384]{1,0:T(8,128)S(1)}) fusion(f32[512]{0:T(512)S(1)} %get-tuple-element.757, f32[512,384]{1,0:T(8,128)S(1)} %copy-done.3, f32[384,3072]{1,0:T(8,128)} %param.21, f32[512,3072]{1,0:T(8,128)} %copy-done.1), kind=kOutput, calls=%fused_computation.44 | convolution fusion | flops 7251295744 | bytes 12586496 | tf_op jit(solution)/shard_map/dot_general | solution.py:98
  675.3 15.4 %fusion.26 = f32[3072,384]{1,0:T(8,128)} fusion(f32[512,384]{1,0:T(8,128)S(1)} %get-tuple-element.761, f32[512,3072]{1,0:T(8,128)} %all-reduce.4.cloned.1.call-done, f32[512,3072]{1,0:T(8,128)} %all-gather.23.cloned.1.call-done, f32[512]{0:T(512)S(1)} %get-tuple-element.757, f32[512]{0:T(512)S(1)} %get-tuple-element.756), kind=kOutput, calls=%fused_computation.76 | convolution fusion | flops 7252475904 | bytes 18092032 | tf_op jit(solution)/shard_map/dot_general | solution.py:106
  690.7 2.1 constant_dynamic-slice_fusion.6
  692.8 10.5 %all-reduce = (f32[384]{0:T(512)}, f32[]{:T(128)}) all-reduce(f32[384]{0:T(512)S(1)} %get-tuple-element.760, f32[]{:T(128)} %get-tuple-element.744), channel_id=1, replica_groups=mesh['row'=4,'col'=8] {'row'}, use_global_device_ids=true, to_apply=%region_26.0 | all-reduce | flops 385 | bytes 3080 | tf_op jit(solution)/shard_map/psum | solution.py:114
  703.9 13.4 %reduce-scatter.5.cloned.1.call-done = f32[384,768]{1,0:T(8,128)} async-done(((f32[384,3072]{1,0:T(8,128)}), f32[384,768]{1,0:T(8,128)}) %reduce-scatter.5.cloned.1.call-update) | async-done | bytes 1179664 | tf_op jit(solution)/shard_map/reduce_scatter | solution.py:112
  717.3 60.4 %reduce-scatter.3.cloned.1.call-done = f32[768,384]{1,0:T(8,128)} async-done(((f32[3072,384]{1,0:T(8,128)}), f32[768,384]{1,0:T(8,128)}) %reduce-scatter.3.cloned.1.call-update) | async-done | bytes 1179664 | tf_op jit(solution)/shard_map/reduce_scatter | solution.py:111
  (127 shorter events, 8.0 us)
Async XLA Ops:
  7.2 69.9 %all-gather.23.cloned.1.call-start = ((), (), s32[]{:S(2)}) async-start(), calls=%async_computation.2 | async-start | bytes 7077888 | tf_op jit(solution)/shard_map/all_gather | solution.py:45
  7.9 165.9 %all-gather.25.cloned.1.call-start = ((), (), s32[]{:S(2)}) async-start(), calls=%async_computation.3 | async-start | bytes 11796480 | tf_op jit(solution)/shard_map/all_gather | solution.py:46
  8.6 464.9 %all-reduce.4.cloned.1.call-start = ((), (), s32[]{:S(2)}) async-start(), calls=%async_computation.4 | async-start | bytes 12582912 | tf_op jit(solution)/shard_map/psum | solution.py:75
  173.8 5.5 copy-start
  266.7 73.1 %copy-start.5 = (f32[512]{0:T(512)}, f32[512]{0:T(512)S(1)}, u32[]{:S(2)}) copy-start(f32[512]{0:T(512)S(1)} %add_subtract_fusion.2) | copy-start | bytes 6148
  293.9 45.8 %copy-start.4 = (f32[768]{0:T(1024)}, f32[768]{0:T(1024)S(1)}, u32[]{:S(2)}) copy-start(f32[768]{0:T(1024)S(1)} %add_subtract_fusion) | copy-start | bytes 9220
  339.8 0.7 copy-start.6
  339.8 133.8 %copy-start.7 = (f32[384]{0:T(512)S(1)}, f32[384]{0:T(512)}, u32[]{:S(2)}) copy-start(f32[384]{0:T(512)} %param.20) | copy-start | bytes 4612
  339.8 149.3 %slice-start = ((s8[4718592]{0:T(1024)(128)(4,1)}), s8[524288]{0:T(1024)(128)(4,1)S(1)}, s32[]{:S(2)}) async-start(s8[4718592]{0:T(1024)(128)(4,1)} %bitcast.67), calls=%async_computation.8 | async-start | bytes 1048576
  339.8 297.5 %all-reduce.6.cloned.1.call-start = ((), (), s32[]{:S(2)}) async-start(), calls=%async_computation.5 | async-start | bytes 12582912 | tf_op jit(solution)/shard_map/psum | solution.py:87
  473.6 15.5 %slice-start.1 = ((s8[4718592]{0:T(1024)(128)(4,1)}), s8[4194304]{0:T(1024)(128)(4,1)S(1)}, s32[]{:S(2)}) async-start(s8[4718592]{0:T(1024)(128)(4,1)} %bitcast.67), calls=%async_computation.9 | async-start | bytes 8388608
  488.2 0.9 copy-start.2
  501.1 216.2 %reduce-scatter.5.cloned.1.call-start = ((), (), s32[]{:S(2)}) async-start(), calls=%async_computation.7 | async-start | bytes 5898240 | tf_op jit(solution)/shard_map/reduce_scatter | solution.py:112
  646.8 2.6 copy-start.1
  660.1 1.1 copy-start.3
  660.1 117.6 %reduce-scatter.3.cloned.1.call-start = ((), (), s32[]{:S(2)}) async-start(), calls=%async_computation.6 | async-start | bytes 5898240 | tf_op jit(solution)/shard_map/reduce_scatter | solution.py:111
Sparse Core Ops, SparseCore 0:
  9.6 67.4 all-gather.22
  78.9 94.8 all-gather.24
  339.9 133.6 all-reduce.3
  501.2 136.0 all-reduce.5
  660.2 57.0 reduce-scatter.4
  720.7 56.9 reduce-scatter.2
where the time goes:
time: 794 us; the launch traced here: 786 us
  waiting for transfers between devices  506 us (64%)
  blocking collectives  129 us (16%)
  matrix products  104 us (13%)
  other arithmetic  20.5 us (3%)
  between operations  16.6 us (2%)
  local copies, waits for them, and re-layouts  8.41 us (1%)
    psum x1, waiting for transfers between devices, body(): out = lax.psum(part_out, 'col')  136 us
    psum x1, waiting for transfers between devices, body(): whole_targets = lax.psum(partial_value, 'col')  133 us
    all_gather x10, blocking collectives, merged(): everything = jax.tree.map(lambda part: lax.all_gather(part, axis), array)  118 us
    all_gather x1, waiting for transfers between devices, body(): full_images = lax.all_gather(images, 'row', axis=1, tiled=True)  93.5 us
    all_gather x1, waiting for transfers between devices, body(): full_noise = lax.all_gather(noise, 'col', axis=1, tiled=True)  68.3 us
    reduce_scatter x1, waiting for transfers between devices, body(): lax.psum_scatter(local_in, 'row', scatter_dimension=0, tiled=True)  60.4 us
    dot_general x1, matrix products, body(): jnp.dot(weights, full_images, precision=highest, preferred_element_type=j...  19.3 us
    dot_general x1, matrix products, body(): lax.dot_general(full_noise, full_images, (((1,), (1,)), ((), ())), precis...  18.3 us
  transfers between devices with their start and end apart: 6, of which 6 were waited for; matrix products, arithmetic and copies ran while one was open for 4% of the time, Pallas kernels for 0%

commit v1 on v0

--- a/solution.py
+++ b/solution.py
@@ -6,6 +6,11 @@
 ITERS = 2
 TIMES = 1000
 EPSILON = 0.01
+
+
+def add_all(array, mesh_axis):
+    pieces = lax.all_gather(array, mesh_axis)
+    return jnp.sum(pieces, axis=0)
 
 
 def merged(array, axis, combine):
@@ -84,7 +89,7 @@
     sigma = jax.nn.sigmoid(pre)
     hidden = pre * sigma
     part_out = jnp.dot(hidden, w_out, precision=highest, preferred_element_type=jnp.float32)
-    out = lax.psum(part_out, "col")
+    out = add_all(part_out, "col")
     diff = out - velocity
     squared = jnp.sum(diff * diff)
     slope = diff / jnp.sqrt(jnp.float32(noise_count))

time: 794 us -> 1110 us (1.40)
  waiting for transfers between devices: 506 us -> 797 us
  other arithmetic: 20.5 us -> 44.9 us
    all_gather x0 -> x1, waiting for transfers between devices: none -> 427 us  [add_all(): pieces = lax.all_gather(array, mesh_axis)]
    psum x1 -> x0, waiting for transfers between devices: 136 us -> none  [body(): out = lax.psum(part_out, 'col')]
    reduce_sum x0 -> x1, other arithmetic: none -> 21.2 us  [add_all(): return jnp.sum(pieces, axis=0)]
  transfers between devices with their start and end apart: 6 -> 6, of which waited for: 6 -> 6; matrix products, arithmetic and copies ran while one was open for 4% -> 3% of each run, Pallas kernels for 0% -> 0%
where the time goes in v1:
time: 1110 us; the launch traced here: 1100 us
  waiting for transfers between devices  797 us (72%)
  blocking collectives  129 us (12%)
  matrix products  105 us (9%)
  other arithmetic  44.9 us (4%)
  between operations  16.6 us (1%)
    all_gather x1, waiting for transfers between devices, add_all(): pieces = lax.all_gather(array, mesh_axis)  427 us
    psum x1, waiting for transfers between devices, body(): whole_targets = lax.psum(partial_value, 'col')  133 us
    all_gather x10, blocking collectives, merged(): everything = jax.tree.map(lambda part: lax.all_gather(part, axis), array)  118 us
    all_gather x1, waiting for transfers between devices, body(): full_images = lax.all_gather(images, 'row', axis=1, tiled=True)  93.5 us
    all_gather x1, waiting for transfers between devices, body(): full_noise = lax.all_gather(noise, 'col', axis=1, tiled=True)  68.3 us
    reduce_scatter x1, waiting for transfers between devices, body(): lax.psum_scatter(local_in, 'row', scatter_dimension=0, tiled=True)  60.4 us
  transfers between devices with their start and end apart: 6, of which 6 were waited for; matrix products, arithmetic and copies ran while one was open for 3% of the time, Pallas kernels for 0%

profile of v1, /device:TPU:0, one launch (start us, length us, event | category | flops | bytes accessed | tf_op | source)
XLA Modules:
  0.0 1097.2 jit_solution(392495603078592700)
XLA Ops:
  7.2 0.7 all-gather.25.cloned.1.call-update
  7.9 0.7 all-gather.27.cloned.1.call-update
  8.7 68.3 %all-gather.25.cloned.1.call-done = f32[512,3072]{1,0:T(8,128)} async-done(((f32[512,384]{1,0:T(8,128)}), f32[512,3072]{1,0:T(8,128)}) %all-gather.25.cloned.1.call-update) | async-done | bytes 6291472 | tf_op jit(solution)/shard_map/all_gather | solution.py:50
  77.0 3.3 multiply_reduce_fusion.2
  80.3 93.5 %all-gather.27.cloned.1.call-done = f32[768,3072]{1,0:T(8,128)} async-done(((f32[768,768]{1,0:T(8,128)}), f32[768,3072]{1,0:T(8,128)}) %all-gather.27.cloned.1.call-update) | async-done | bytes 9437200 | tf_op jit(solution)/shard_map/all_gather | solution.py:51
  173.8 4.5 multiply_reduce_fusion
  178.3 1.0 copy-done
  179.2 18.3 %subtract_reduce_fusion.3 = (f32[512]{0:T(512)S(1)}, f32[512,768]{1,0:T(8,128)S(1)}) fusion(f32[512,3072]{1,0:T(8,128)S(1)} %copy-done, f32[768,3072]{1,0:T(8,128)} %all-gather.27.cloned.1.call-done, f32[768]{0:T(1024)S(1)} %multiply_reduce_fusion, f32[512]{0:T(512)S(1)} %multiply_reduce_fusion.2), kind=kOutput, calls=%fused_computation.38 | convolution fusion | flops 14497873920 | bytes 17308672 | tf_op jit(solution)/shard_map/dot_general | solution.py:57
  197.9 12.8 %all-gather.12 = f32[8,1,512]{2,1,0:T(1,128)S(1)} all-gather(f32[1,1,512]{2,1,0:T(1,128)S(1)} %bitcast.97), channel_id=3, replica_groups=mesh['row'=4,'col'=8] {'col'}, dimensions={0}, use_global_device_ids=true | all-gather | bytes 18432 | tf_op jit(solution)/shard_map/all_gather | solution.py:17
  210.8 12.8 %all-gather.11 = f32[8,1,512]{2,1,0:T(1,128)S(1)} all-gather(f32[1,1,512]{2,1,0:T(1,128)S(1)} %bitcast.95), channel_id=2, replica_groups=mesh['row'=4,'col'=8] {'col'}, dimensions={0}, use_global_device_ids=true | all-gather | bytes 18432 | tf_op jit(solution)/shard_map/all_gather | solution.py:17
  224.5 8.1 all-gather.14
  232.6 7.2 all-gather.13
  240.7 12.8 %all-gather.16 = f32[8,1,512]{2,1,0:T(1,128)S(1)} all-gather(f32[1,1,512]{2,1,0:T(1,128)S(1)} %bitcast.96), channel_id=7, replica_groups=mesh['row'=4,'col'=8] {'col'}, dimensions={0}, use_global_device_ids=true | all-gather | bytes 18432 | tf_op jit(solution)/shard_map/all_gather | solution.py:17
  253.5 12.8 %all-gather.15 = f32[8,1,512]{2,1,0:T(1,128)S(1)} all-gather(f32[1,1,512]{2,1,0:T(1,128)S(1)} %bitcast.93), channel_id=6, replica_groups=mesh['row'=4,'col'=8] {'col'}, dimensions={0}, use_global_device_ids=true | all-gather | bytes 18432 | tf_op jit(solution)/shard_map/all_gather | solution.py:17
  267.2 8.1 all-gather.18
  275.4 18.3 %all-gather.17 = f32[4,1,768]{2,1,0:T(1,128)S(1)} all-gather(f32[1,1,768]{2,1,0:T(1,128)S(1)} %reshape.72), channel_id=8, replica_groups=mesh['row'=4,'col'=8] {'row'}, dimensions={0}, use_global_device_ids=true | all-gather | bytes 15360 | tf_op jit(solution)/shard_map/all_gather | solution.py:17
  294.5 12.8 %all-gather.20 = f32[8,1,512]{2,1,0:T(1,128)S(1)} all-gather(f32[1,1,512]{2,1,0:T(1,128)S(1)} %bitcast.98), channel_id=11, replica_groups=mesh['row'=4,'col'=8] {'col'}, dimensions={0}, use_global_device_ids=true | all-gather | bytes 18432 | tf_op jit(solution)/shard_map/all_gather | solution.py:17
  307.3 12.8 %all-gather.19 = f32[8,1,512]{2,1,0:T(1,128)S(1)} all-gather(f32[1,1,512]{2,1,0:T(1,128)S(1)} %bitcast.94), channel_id=10, replica_groups=mesh['row'=4,'col'=8] {'col'}, dimensions={0}, use_global_device_ids=true | all-gather | bytes 18432 | tf_op jit(solution)/shard_map/all_gather | solution.py:17
  320.5 19.3 %fusion.6 = f32[512,3072]{1,0:T(8,128)} fusion(f32[768,3072]{1,0:T(8,128)} %all-gather.27.cloned.1.call-done, f32[512,768]{1,0:T(8,128)S(1)} %get-tuple-element.759, f32[512]{0:T(512)S(1)} %log_add_fusion, f32[768]{0:T(1024)S(1)} %add_subtract_fusion), kind=kOutput, calls=%fused_computation.26 | convolution fusion | flops 14496301056 | bytes 17306624 | tf_op jit(solution)/shard_map/dot_general | solution.py:75
  340.4 133.1 %all-reduce.3.cloned.1.call-done = f32[512,3072]{1,0:T(8,128)} async-done(((f32[512,3072]{1,0:T(8,128)}), f32[512,3072]{1,0:T(8,128)}) %all-reduce.3.cloned.1.call-update) | async-done | bytes 6291472 | tf_op jit(solution)/shard_map/psum | solution.py:80
  473.6 14.5 %convolution_add_fusion = f32[512,384]{1,0:T(8,128)S(1)} fusion(f32[3072,384]{1,0:T(8,128)} %param.19, f32[384]{0:T(512)S(1)} %copy-done.4, f32[512]{0:T(512)S(1)} %get-tuple-element.757, f32[512,3072]{1,0:T(8,128)} %all-reduce.3.cloned.1.call-done, f32[512,3072]{1,0:T(8,128)} %all-gather.25.cloned.1.call-done, f32[512]{0:T(512)S(1)} %get-tuple-element.756), kind=kOutput, calls=%fused_computation.43 | convolution fusion | flops 7252869120 | bytes 18093568 | tf_op jit(solution)/shard_map/dot_general | solution.py:86
  488.1 12.0 %fusion.20 = f32[512,3072]{1,0:T(8,128)} fusion(f32[384,3072]{1,0:T(8,128)S(1)} %bitcast.70, f32[512,384]{1,0:T(8,128)S(1)} %convolution_add_fusion), kind=kOutput, calls=%fused_computation.49 | convolution fusion | flops 7248543744 | bytes 11796480 | tf_op jit(solution)/shard_map/dot_general | solution.py:91
  500.4 427.3 %all-gather.29.cloned.1.call-done = f32[4096,3072]{1,0:T(8,128)} async-done(((f32[512,3072]{1,0:T(8,128)}), f32[4096,3072]{1,0:T(8,128)}) %all-gather.29.cloned.1.call-update) | async-done | bytes 50331664 | tf_op jit(solution)/shard_map/all_gather | solution.py:12
  927.8 21.2 %reduce_sum.97 = f32[512,3072]{1,0:T(8,128)} reduce(f32[8,512,3072]{2,1,0:T(8,128)} %bitcast.68, f32[]{:T(128)} %constant.202.clone.1), dimensions={0}, to_apply=%region_23.0 | reduce | flops 11010048 | bytes 56623108 | tf_op jit(solution)/shard_map/reduce_sum | solution.py:13
  949.0 12.7 %multiply_reduce_fusion.1 = (f32[]{:T(128)}, f32[512,3072]{1,0:T(8,128)}) fusion(f32[512,3072]{1,0:T(8,128)} %reduce_sum.97, f32[512,3072]{1,0:T(8,128)} %all-reduce.3.cloned.1.call-done, f32[512,3072]{1,0:T(8,128)} %all-gather.25.cloned.1.call-done), kind=kLoop, calls=%fused_computation.16 | loop fusion | flops 6291455 | bytes 25165828 | tf_op jit(solution)/shard_map/reduce_sum | solution.py:94
  961.7 11.3 %fusion = f32[384,3072]{1,0:T(8,128)} fusion(f32[512,3072]{1,0:T(8,128)} %get-tuple-element.745, f32[512,384]{1,0:T(8,128)S(1)} %convolution_add_fusion), kind=kOutput, calls=%fused_computation.20 | convolution fusion | flops 7250116608 | bytes 11796480 | tf_op jit(solution)/shard_map/dot_general | solution.py:96
  973.4 14.1 %multiply_reduce_fusion.3 = (f32[384]{0:T(512)S(1)}, f32[512,384]{1,0:T(8,128)S(1)}) fusion(f32[512]{0:T(512)S(1)} %get-tuple-element.757, f32[512,384]{1,0:T(8,128)S(1)} %convolution_add_fusion, f32[384,3072]{1,0:T(8,128)} %param.21, f32[512,3072]{1,0:T(8,128)} %get-tuple-element.745), kind=kOutput, calls=%fused_computation.44 | convolution fusion | flops 7251295744 | bytes 12586496 | tf_op jit(solution)/shard_map/dot_general | solution.py:103
  987.4 15.4 %fusion.26 = f32[3072,384]{1,0:T(8,128)} fusion(f32[512,384]{1,0:T(8,128)S(1)} %get-tuple-element.761, f32[512,3072]{1,0:T(8,128)} %all-reduce.3.cloned.1.call-done, f32[512,3072]{1,0:T(8,128)} %all-gather.25.cloned.1.call-done, f32[512]{0:T(512)S(1)} %get-tuple-element.757, f32[512]{0:T(512)S(1)} %get-tuple-element.756), kind=kOutput, calls=%fused_computation.76 | convolution fusion | flops 7252475904 | bytes 18092032 | tf_op jit(solution)/shard_map/dot_general | solution.py:111
  1002.8 2.1 constant_dynamic-slice_fusion.6
  1004.9 10.4 all-reduce
  1016.0 12.5 %reduce-scatter.5.cloned.1.call-done = f32[384,768]{1,0:T(8,128)} async-done(((f32[384,3072]{1,0:T(8,128)}), f32[384,768]{1,0:T(8,128)}) %reduce-scatter.5.cloned.1.call-update) | async-done | bytes 1179664 | tf_op jit(solution)/shard_map/reduce_scatter | solution.py:117
  1028.4 60.4 %reduce-scatter.3.cloned.1.call-done = f32[768,384]{1,0:T(8,128)} async-done(((f32[3072,384]{1,0:T(8,128)}), f32[768,384]{1,0:T(8,128)}) %reduce-scatter.3.cloned.1.call-update) | async-done | bytes 1179664 | tf_op jit(solution)/shard_map/reduce_scatter | solution.py:116
  (122 shorter events, 6.6 us)
Async XLA Ops:
  7.2 69.9 %all-gather.25.cloned.1.call-start = ((), (), s32[]{:S(2)}) async-start(), calls=%async_computation.2 | async-start | bytes 7077888 | tf_op jit(solution)/shard_map/all_gather | solution.py:50
  7.9 165.9 %all-gather.27.cloned.1.call-start = ((), (), s32[]{:S(2)}) async-start(), calls=%async_computation.3 | async-start | bytes 11796480 | tf_op jit(solution)/shard_map/all_gather | solution.py:51
  8.6 464.9 %all-reduce.3.cloned.1.call-start = ((), (), s32[]{:S(2)}) async-start(), calls=%async_computation.4 | async-start | bytes 12582912 | tf_op jit(solution)/shard_map/psum | solution.py:80
  173.8 5.5 copy-start
  266.6 73.1 %copy-start.2 = (f32[512]{0:T(512)}, f32[512]{0:T(512)S(1)}, u32[]{:S(2)}) copy-start(f32[512]{0:T(512)S(1)} %add_subtract_fusion.2) | copy-start | bytes 6148
  293.9 45.8 %copy-start.1 = (f32[768]{0:T(1024)}, f32[768]{0:T(1024)S(1)}, u32[]{:S(2)}) copy-start(f32[768]{0:T(1024)S(1)} %add_subtract_fusion) | copy-start | bytes 9220
  339.7 0.7 copy-start.3
  339.7 133.8 %copy-start.4 = (f32[384]{0:T(512)S(1)}, f32[384]{0:T(512)}, u32[]{:S(2)}) copy-start(f32[384]{0:T(512)} %param.20) | copy-start | bytes 4612
  339.8 148.3 %slice-start = ((s8[4718592]{0:T(1024)(128)(4,1)}), s8[524288]{0:T(1024)(128)(4,1)S(1)}, s32[]{:S(2)}) async-start(s8[4718592]{0:T(1024)(128)(4,1)} %bitcast.69), calls=%async_computation.8 | async-start | bytes 1048576
  339.8 588.0 %all-gather.29.cloned.1.call-start = ((), (), s32[]{:S(2)}) async-start(), calls=%async_computation.7 | async-start | bytes 56623104 | tf_op jit(solution)/shard_map/all_gather | solution.py:12
  473.6 14.5 %slice-start.1 = ((s8[4718592]{0:T(1024)(128)(4,1)}), s8[4194304]{0:T(1024)(128)(4,1)S(1)}, s32[]{:S(2)}) async-start(s8[4718592]{0:T(1024)(128)(4,1)} %bitcast.69), calls=%async_computation.9 | async-start | bytes 8388608
  500.2 528.2 %reduce-scatter.5.cloned.1.call-start = ((), (), s32[]{:S(2)}) async-start(), calls=%async_computation.6 | async-start | bytes 5898240 | tf_op jit(solution)/shard_map/reduce_scatter | solution.py:117
  973.1 115.7 %reduce-scatter.3.cloned.1.call-start = ((), (), s32[]{:S(2)}) async-start(), calls=%async_computation.5 | async-start | bytes 5898240 | tf_op jit(solution)/shard_map/reduce_scatter | solution.py:116
Sparse Core Ops, SparseCore 0:
  9.6 67.4 all-gather.24
  78.9 94.8 all-gather.26
  339.9 133.6 all-reduce.2
  500.3 427.4 all-gather.28
  973.2 55.1 reduce-scatter.4
  1031.8 56.9 reduce-scatter.2
